TPU v7x, 32 devices: a whole 2x2x4 slice. The times are simulated.
32 devices in a mesh: row: 8 (over z, x), col: 4 (over y, core).
Axes of the slice: x: 2, y: 2, z: 4, core: 2. Of those that a mesh axis runs over, the one named last changes fastest.
Arguments:
- positions: float32 [3, 8192], P(None, ('row', 'col')), may hold values from -6 to 6
- features: bfloat16 [128, 8192], P(None, ('row', 'col')), may hold values from -6 to 6
- fill: int32 [64], P(('row', 'col')), may hold values from 64 to 128, as said below
- tiles: int32 [256, 2], P(('row', 'col')), may hold values from 0 to 15, as said below
- tile_count: int32 [32], P(('row', 'col')), may hold values from 2 to 8, as said below
- w_radial: float32 [64, 32], replicated, may hold values from -1 to 1
- w_left: bfloat16 [128, 64], replicated, may hold values from -0.5 to 0.5
- w_right: bfloat16 [128, 64], replicated, may hold values from -0.5 to 0.5
- w_hidden: bfloat16 [64, 64], replicated, may hold values from -0.75 to 0.75
- w_out: bfloat16 [64], replicated, may hold values from -0.25 to 0.25
Outputs:
- forces: float32 [3, 8192], P(None, ('row', 'col'))
- bead_energy: float32 [8192], P(('row', 'col'))
Inputs may be any that keep to these rules, and one draw needn't show every extreme that they name: `fill`: at least 64; some cluster holds 128. `tiles`: A device's 8 slots name distinct cluster pairs; the first entry is below 8, the second below 16; some device has the pair of the last clusters of both groups. `tile_count`: at least 2; some device has all 8 slots live.
All inputs are finite; a program needn't handle non-finite values.
Results may differ from a plain program's by a relative error of at most 0.0045.
Values may be sent and summed in bfloat16 or wider, within the bound.
A program may use at most 64 MiB of HBM per device.

v0:
```python
import jax
import jax.numpy as jnp
from jax import lax
from jax.sharding import PartitionSpec as P

CL = 128
CPD = 2


SOFT = 0.01
RANGE = 6.0


def dsilu(value):
    sig = jax.nn.sigmoid(value)
    return sig * (1.0 + value * (1.0 - sig))


def tile_terms(left, right, proj_a, proj_b, same, live_tile, w_radial, w_hidden, w_out):
    slots = left.shape[1]
    hidden = w_radial.shape[0]
    nbasis = w_radial.shape[1]
    delta = left[:3, :, None] - right[:3, None, :]
    dist = jnp.sqrt(jnp.sum(delta * delta, 0) + SOFT)
    ident = (jnp.arange(slots)[:, None] == jnp.arange(slots)[None, :]).astype(jnp.float32)
    mask = left[3][:, None] * right[3][None, :] * (1.0 - same * ident) * live_tile
    flat = dist.reshape(-1)
    centers = RANGE * jnp.arange(nbasis, dtype=jnp.float32) / (nbasis - 1)
    sharp = ((nbasis - 1) / RANGE) ** 2
    offset = flat[None, :] - centers[:, None]
    basis = jnp.exp(-sharp * offset * offset)
    pair_in = (
        proj_a.astype(jnp.float32)[:, :, None] + proj_b.astype(jnp.float32)[:, None, :]
    ).reshape(hidden, -1)
    pre1 = jnp.dot(w_radial, basis, precision=lax.Precision.HIGHEST) + pair_in
    act1 = jax.nn.silu(pre1).astype(jnp.bfloat16)
    pre2 = jnp.dot(w_hidden, act1, preferred_element_type=jnp.float32)
    act2 = jax.nn.silu(pre2).astype(jnp.bfloat16)
    energy = jnp.dot(w_out[None, :], act2, preferred_element_type=jnp.float32)[0]
    back2 = (w_out.astype(jnp.float32)[:, None] * dsilu(pre2)).astype(jnp.bfloat16)
    back1 = lax.dot_general(
        w_hidden, back2, (((0,), (0,)), ((), ())), preferred_element_type=jnp.float32
    ) * dsilu(pre1)
    radial = lax.dot_general(
        w_radial, back1, (((0,), (0,)), ((), ())), precision=lax.Precision.HIGHEST
    )
    slope = jnp.sum(radial * basis * (-2.0 * sharp * offset), 0)
    weight = mask * slope.reshape(slots, slots) / dist
    energy_left = jnp.sum(mask * energy.reshape(slots, slots), 1)
    pos_left = left[:3]
    pos_right = right[:3]
    force_left = (
        jnp.dot(pos_right, weight.T, precision=lax.Precision.HIGHEST)
        - pos_left * jnp.sum(weight, 1)[None, :]
    )
    force_right = (
        jnp.dot(pos_left, weight, precision=lax.Precision.HIGHEST)
        - pos_right * jnp.sum(weight, 0)[None, :]
    )
    return (force_left, energy_left, force_right)


def project(weight, descriptors):
    return lax.dot_general(
        weight, descriptors, (((0,), (0,)), ((), ())), preferred_element_type=jnp.float32
    ).astype(jnp.bfloat16)


def body(positions, features, fill, tiles, tile_count, w_radial, w_left, w_right, w_hidden, w_out):
    beads = positions.shape[1]
    live = (
        (jnp.arange(CL, dtype=jnp.int32)[None, :] < fill[:, None])
        .astype(jnp.float32)
        .reshape(beads)
    )
    coords = jnp.concatenate([positions, live[None, :]], 0)
    row_coords = lax.all_gather(coords, "col", axis=1, tiled=True)
    col_coords = lax.all_gather(coords, "row", axis=1, tiled=True)
    row_proj = lax.all_gather(project(w_left, features), "col", axis=1, tiled=True)
    col_proj = lax.all_gather(project(w_right, features), "row", axis=1, tiled=True)
    row_index = lax.axis_index("row")
    col_index = lax.axis_index("col")
    col_count = lax.axis_size("col")
    row_base = row_index * col_count * CPD
    live_count = tile_count[0]

    def step(slot, carry):
        firsts, seconds = carry
        first = tiles[slot, 0]
        other = tiles[slot, 1]
        global_a = row_base + first
        global_b = (other // CPD * col_count + col_index) * CPD + other % CPD
        same = (global_a == global_b).astype(jnp.float32)
        live_tile = (slot < live_count).astype(jnp.float32)
        start_a = first * CL
        start_b = other * CL
        left = lax.dynamic_slice_in_dim(row_coords, start_a, CL, 1)
        right = lax.dynamic_slice_in_dim(col_coords, start_b, CL, 1)
        part_a = lax.dynamic_slice_in_dim(row_proj, start_a, CL, 1)
        part_b = lax.dynamic_slice_in_dim(col_proj, start_b, CL, 1)
        force_a, energy_a, force_b = tile_terms(
            left, right, part_a, part_b, same, live_tile, w_radial, w_hidden, w_out
        )
        added = jnp.concatenate([force_a, energy_a[None, :]], 0)
        firsts = lax.dynamic_update_slice_in_dim(
            firsts, lax.dynamic_slice_in_dim(firsts, start_a, CL, 1) + added, start_a, 1
        )
        seconds = lax.dynamic_update_slice_in_dim(
            seconds, lax.dynamic_slice_in_dim(seconds, start_b, CL, 1) + force_b, start_b, 1
        )
        return (firsts, seconds)

    start = (
        jnp.zeros((4, row_coords.shape[1]), jnp.float32),
        jnp.zeros((3, col_coords.shape[1]), jnp.float32),
    )
    firsts, seconds = lax.fori_loop(0, tiles.shape[0], step, start)
    row_part = lax.psum_scatter(firsts, "col", scatter_dimension=1, tiled=True)
    col_part = lax.psum_scatter(seconds, "row", scatter_dimension=1, tiled=True)
    return (row_part[:3] + col_part, row_part[3])


def solution(mesh):
    return jax.shard_map(
        body,
        mesh=mesh,
        in_specs=(
            P(None, ("row", "col")),
            P(None, ("row", "col")),
            P(("row", "col")),
            P(("row", "col"), None),
            P(("row", "col")),
            P(),
            P(),
            P(),
            P(),
            P(),
        ),
        out_specs=(P(None, ("row", "col")), P(("row", "col"))),
        check_vma=False,
    )
```

profile of v0, /device:TPU:0, one launch (start us, length us, event | category | flops | bytes accessed | tf_op | source)
XLA Modules:
  0.0 370.9 jit_solution(6383089554547883600)
XLA Ops:
  8.6 32.4 %all_gather.12 = f32[4,2048]{1,0:T(4,128)S(1)} all-gather(f32[4,256]{1,0:T(4,128)S(1)} %pad_maximum_fusion), channel_id=1, replica_groups=mesh['row'=8,'col'=4] {'row'}, dimensions={1}, use_global_device_ids=true | all-gather | bytes 36864 | tf_op jit(solution)/shard_map/all_gather | solution.py:78
  41.1 5.2 %all_gather.13 = f32[4,1024]{1,0:T(4,128)S(1)} all-gather(f32[4,256]{1,0:T(4,128)S(1)} %pad_maximum_fusion), channel_id=1, replica_groups=mesh['row'=8,'col'=4] {'col'}, dimensions={1}, use_global_device_ids=true | all-gather | bytes 20480 | tf_op jit(solution)/shard_map/all_gather | solution.py:77
  47.1 30.8 %all_gather.15 = bf16[64,2048]{1,0:T(8,128)(2,1)S(1)} all-gather(bf16[64,256]{1,0:T(8,128)(2,1)S(1)} %convolution_convert_fusion), channel_id=1, replica_groups=mesh['row'=8,'col'=4] {'row'}, dimensions={1}, use_global_device_ids=true | all-gather | bytes 294912 | tf_op jit(solution)/shard_map/all_gather | solution.py:80
  78.8 5.4 %all_gather.14 = bf16[64,1024]{1,0:T(8,128)(2,1)S(1)} all-gather(bf16[64,256]{1,0:T(8,128)(2,1)S(1)} %convolution_convert_fusion.1), channel_id=1, replica_groups=mesh['row'=8,'col'=4] {'col'}, dimensions={1}, use_global_device_ids=true | all-gather | bytes 163840 | tf_op jit(solution)/shard_map/all_gather | solution.py:79
  84.2 186.5 %while.17 = (s32[]{:T(128)}, f32[4,1024]{1,0:T(4,128)S(1)}, f32[3,2048]{1,0:T(4,128)S(1)}, s32[8,2]{0,1:T(2,128)}, f32[4,2048]{1,0:T(4,128)S(1)}, /*index=5*/f32...) while((s32[]{:T(128)}, f32[4,1024]{1,0:T(4,128)S(1)}, ...), condition=%wide.region_6.7_spmd, body=%wide.region_0.6_spmd.sunk | while | flops 1113033216 | bytes 43096368 | solution.py:117
  88.2 5.9 %fusion.85 = f32[64,16384]{1,0:T(8,128)S(1)} fusion(f32[64,32]{0,1:T(8,128)S(1)} %copy-done.1, f32[8,8,128,128]{3,2,1,0:T(8,128)S(1)} %bitcast.136, f32[32]{0:T(128)S(1)} %iota_multiply_fusion.2, f32[16384]{0:T(1024)S(1)} %sqrt_bitcast_fusion.2), kind=kOutput, calls=%fused_computation.3.clone.1 | convolution fusion | flops 405274624 | bytes 8462464 | tf_op jit(solution)/shard_map/while/body/eval_jaxpr/dot_general | solution.py:35
  95.8 3.4 fusion.87
  99.2 2.9 fusion.88
  111.5 5.9 %fusion.85 = f32[64,16384]{1,0:T(8,128)S(1)} fusion(f32[64,32]{0,1:T(8,128)S(1)} %copy-done.1, f32[8,8,128,128]{3,2,1,0:T(8,128)S(1)} %bitcast.136, f32[32]{0:T(128)S(1)} %iota_multiply_fusion.2, f32[16384]{0:T(1024)S(1)} %sqrt_bitcast_fusion.2), kind=kOutput, calls=%fused_computation.3.clone.1 | convolution fusion | flops 405274624 | bytes 8462464 | tf_op jit(solution)/shard_map/while/body/eval_jaxpr/dot_general | solution.py:35
  119.1 3.4 fusion.87
  134.8 5.9 %fusion.85 = f32[64,16384]{1,0:T(8,128)S(1)} fusion(f32[64,32]{0,1:T(8,128)S(1)} %copy-done.1, f32[8,8,128,128]{3,2,1,0:T(8,128)S(1)} %bitcast.136, f32[32]{0:T(128)S(1)} %iota_multiply_fusion.2, f32[16384]{0:T(1024)S(1)} %sqrt_bitcast_fusion.2), kind=kOutput, calls=%fused_computation.3.clone.1 | convolution fusion | flops 405274624 | bytes 8462464 | tf_op jit(solution)/shard_map/while/body/eval_jaxpr/dot_general | solution.py:35
  142.4 3.4 fusion.87
  158.2 5.9 %fusion.85 = f32[64,16384]{1,0:T(8,128)S(1)} fusion(f32[64,32]{0,1:T(8,128)S(1)} %copy-done.1, f32[8,8,128,128]{3,2,1,0:T(8,128)S(1)} %bitcast.136, f32[32]{0:T(128)S(1)} %iota_multiply_fusion.2, f32[16384]{0:T(1024)S(1)} %sqrt_bitcast_fusion.2), kind=kOutput, calls=%fused_computation.3.clone.1 | convolution fusion | flops 405274624 | bytes 8462464 | tf_op jit(solution)/shard_map/while/body/eval_jaxpr/dot_general | solution.py:35
  165.7 3.4 fusion.87
  181.5 5.9 %fusion.85 = f32[64,16384]{1,0:T(8,128)S(1)} fusion(f32[64,32]{0,1:T(8,128)S(1)} %copy-done.1, f32[8,8,128,128]{3,2,1,0:T(8,128)S(1)} %bitcast.136, f32[32]{0:T(128)S(1)} %iota_multiply_fusion.2, f32[16384]{0:T(1024)S(1)} %sqrt_bitcast_fusion.2), kind=kOutput, calls=%fused_computation.3.clone.1 | convolution fusion | flops 405274624 | bytes 8462464 | tf_op jit(solution)/shard_map/while/body/eval_jaxpr/dot_general | solution.py:35
  189.0 3.4 fusion.87
  204.8 5.9 %fusion.85 = f32[64,16384]{1,0:T(8,128)S(1)} fusion(f32[64,32]{0,1:T(8,128)S(1)} %copy-done.1, f32[8,8,128,128]{3,2,1,0:T(8,128)S(1)} %bitcast.136, f32[32]{0:T(128)S(1)} %iota_multiply_fusion.2, f32[16384]{0:T(1024)S(1)} %sqrt_bitcast_fusion.2), kind=kOutput, calls=%fused_computation.3.clone.1 | convolution fusion | flops 405274624 | bytes 8462464 | tf_op jit(solution)/shard_map/while/body/eval_jaxpr/dot_general | solution.py:35
  212.3 3.4 fusion.87
  228.1 5.9 %fusion.85 = f32[64,16384]{1,0:T(8,128)S(1)} fusion(f32[64,32]{0,1:T(8,128)S(1)} %copy-done.1, f32[8,8,128,128]{3,2,1,0:T(8,128)S(1)} %bitcast.136, f32[32]{0:T(128)S(1)} %iota_multiply_fusion.2, f32[16384]{0:T(1024)S(1)} %sqrt_bitcast_fusion.2), kind=kOutput, calls=%fused_computation.3.clone.1 | convolution fusion | flops 405274624 | bytes 8462464 | tf_op jit(solution)/shard_map/while/body/eval_jaxpr/dot_general | solution.py:35
  235.7 3.4 fusion.87
  251.4 5.9 %fusion.85 = f32[64,16384]{1,0:T(8,128)S(1)} fusion(f32[64,32]{0,1:T(8,128)S(1)} %copy-done.1, f32[8,8,128,128]{3,2,1,0:T(8,128)S(1)} %bitcast.136, f32[32]{0:T(128)S(1)} %iota_multiply_fusion.2, f32[16384]{0:T(1024)S(1)} %sqrt_bitcast_fusion.2), kind=kOutput, calls=%fused_computation.3.clone.1 | convolution fusion | flops 405274624 | bytes 8462464 | tf_op jit(solution)/shard_map/while/body/eval_jaxpr/dot_general | solution.py:35
  259.0 3.4 fusion.87
  273.3 21.2 %reduce-scatter.7.cloned.1.call-done = f32[256,4]{1,0:T(8,128)} async-done(((f32[1024,4]{1,0:T(8,128)}), f32[256,4]{1,0:T(8,128)}) %reduce-scatter.7.cloned.1.call-update) | async-done | bytes 4112
  297.1 65.4 %reduce-scatter.9.cloned.1.call-done = f32[256,3]{1,0:T(8,128)} async-done(((f32[2048,3]{1,0:T(8,128)}), f32[256,3]{1,0:T(8,128)}) %reduce-scatter.9.cloned.1.call-update) | async-done | bytes 3088
  (202 shorter events, 79.3 us)
Async XLA Ops:
  7.2 39.1 %copy-start = (bf16[128,256]{1,0:T(8,128)(2,1)S(1)}, bf16[128,256]{1,0:T(8,128)(2,1)}, u32[]{:S(2)}) copy-start(bf16[128,256]{1,0:T(8,128)(2,1)} %param.13) | copy-start | bytes 196612
  7.2 287.3 %reduce-scatter.7.cloned.1.call-start = ((), (), s32[]{:S(2)}) async-start(), calls=%async_computation.2 | async-start | bytes 655360
  84.2 4.0 %copy-start.1 = (f32[64,32]{0,1:T(8,128)S(1)}, f32[64,32]{0,1:T(8,128)}, u32[]{:S(2)}) copy-start(f32[64,32]{0,1:T(8,128)} %get-tuple-element.536) | copy-start | bytes 24580 | tf_op jit(solution)/shard_map/while
  88.2 5.9 %copy-start.2 = (bf16[64,64]{1,0:T(8,128)(2,1)S(1)}, bf16[64,64]{1,0:T(8,128)(2,1)}, u32[]{:S(2)}) copy-start(bf16[64,64]{1,0:T(8,128)(2,1)} %get-tuple-element.539) | copy-start | bytes 24580 | tf_op jit(solution)/shard_map/while
  94.1 1.6 copy-start.3
  107.5 4.0 %copy-start.1 = (f32[64,32]{0,1:T(8,128)S(1)}, f32[64,32]{0,1:T(8,128)}, u32[]{:S(2)}) copy-start(f32[64,32]{0,1:T(8,128)} %get-tuple-element.536) | copy-start | bytes 24580 | tf_op jit(solution)/shard_map/while
  111.5 5.9 %copy-start.2 = (bf16[64,64]{1,0:T(8,128)(2,1)S(1)}, bf16[64,64]{1,0:T(8,128)(2,1)}, u32[]{:S(2)}) copy-start(bf16[64,64]{1,0:T(8,128)(2,1)} %get-tuple-element.539) | copy-start | bytes 24580 | tf_op jit(solution)/shard_map/while
  117.4 1.6 copy-start.3
  130.8 4.0 %copy-start.1 = (f32[64,32]{0,1:T(8,128)S(1)}, f32[64,32]{0,1:T(8,128)}, u32[]{:S(2)}) copy-start(f32[64,32]{0,1:T(8,128)} %get-tuple-element.536) | copy-start | bytes 24580 | tf_op jit(solution)/shard_map/while
  134.8 5.9 %copy-start.2 = (bf16[64,64]{1,0:T(8,128)(2,1)S(1)}, bf16[64,64]{1,0:T(8,128)(2,1)}, u32[]{:S(2)}) copy-start(bf16[64,64]{1,0:T(8,128)(2,1)} %get-tuple-element.539) | copy-start | bytes 24580 | tf_op jit(solution)/shard_map/while
  140.8 1.6 copy-start.3
  154.2 4.0 %copy-start.1 = (f32[64,32]{0,1:T(8,128)S(1)}, f32[64,32]{0,1:T(8,128)}, u32[]{:S(2)}) copy-start(f32[64,32]{0,1:T(8,128)} %get-tuple-element.536) | copy-start | bytes 24580 | tf_op jit(solution)/shard_map/while
  158.1 5.9 %copy-start.2 = (bf16[64,64]{1,0:T(8,128)(2,1)S(1)}, bf16[64,64]{1,0:T(8,128)(2,1)}, u32[]{:S(2)}) copy-start(bf16[64,64]{1,0:T(8,128)(2,1)} %get-tuple-element.539) | copy-start | bytes 24580 | tf_op jit(solution)/shard_map/while
  177.5 4.0 %copy-start.1 = (f32[64,32]{0,1:T(8,128)S(1)}, f32[64,32]{0,1:T(8,128)}, u32[]{:S(2)}) copy-start(f32[64,32]{0,1:T(8,128)} %get-tuple-element.536) | copy-start | bytes 24580 | tf_op jit(solution)/shard_map/while
  181.5 5.9 %copy-start.2 = (bf16[64,64]{1,0:T(8,128)(2,1)S(1)}, bf16[64,64]{1,0:T(8,128)(2,1)}, u32[]{:S(2)}) copy-start(bf16[64,64]{1,0:T(8,128)(2,1)} %get-tuple-element.539) | copy-start | bytes 24580 | tf_op jit(solution)/shard_map/while
  187.4 1.6 copy-start.3
  200.8 4.0 %copy-start.1 = (f32[64,32]{0,1:T(8,128)S(1)}, f32[64,32]{0,1:T(8,128)}, u32[]{:S(2)}) copy-start(f32[64,32]{0,1:T(8,128)} %get-tuple-element.536) | copy-start | bytes 24580 | tf_op jit(solution)/shard_map/while
  204.8 5.9 %copy-start.2 = (bf16[64,64]{1,0:T(8,128)(2,1)S(1)}, bf16[64,64]{1,0:T(8,128)(2,1)}, u32[]{:S(2)}) copy-start(bf16[64,64]{1,0:T(8,128)(2,1)} %get-tuple-element.539) | copy-start | bytes 24580 | tf_op jit(solution)/shard_map/while
  210.7 1.6 copy-start.3
  224.1 4.0 %copy-start.1 = (f32[64,32]{0,1:T(8,128)S(1)}, f32[64,32]{0,1:T(8,128)}, u32[]{:S(2)}) copy-start(f32[64,32]{0,1:T(8,128)} %get-tuple-element.536) | copy-start | bytes 24580 | tf_op jit(solution)/shard_map/while
  228.1 5.9 %copy-start.2 = (bf16[64,64]{1,0:T(8,128)(2,1)S(1)}, bf16[64,64]{1,0:T(8,128)(2,1)}, u32[]{:S(2)}) copy-start(bf16[64,64]{1,0:T(8,128)(2,1)} %get-tuple-element.539) | copy-start | bytes 24580 | tf_op jit(solution)/shard_map/while
  247.4 4.0 %copy-start.1 = (f32[64,32]{0,1:T(8,128)S(1)}, f32[64,32]{0,1:T(8,128)}, u32[]{:S(2)}) copy-start(f32[64,32]{0,1:T(8,128)} %get-tuple-element.536) | copy-start | bytes 24580 | tf_op jit(solution)/shard_map/while
  251.4 5.9 %copy-start.2 = (bf16[64,64]{1,0:T(8,128)(2,1)S(1)}, bf16[64,64]{1,0:T(8,128)(2,1)}, u32[]{:S(2)}) copy-start(bf16[64,64]{1,0:T(8,128)(2,1)} %get-tuple-element.539) | copy-start | bytes 24580 | tf_op jit(solution)/shard_map/while
  271.8 90.6 %reduce-scatter.9.cloned.1.call-start = ((), (), s32[]{:S(2)}) async-start(), calls=%async_computation.3 | async-start | bytes 1179648
  (3 other events, 4.8 us)
Sparse Core Ops, SparseCore 0:
  271.9 22.4 reduce-scatter.6
  297.9 64.5 reduce-scatter.8
where the time goes:
time: 372 us; the launch traced here: 371 us
  matrix products  125 us (34%)
  waiting for transfers between devices  86.6 us (23%)
  blocking collectives  73.9 us (20%)
  loops' own time  39.4 us (11%)
  local copies, waits for them, and re-layouts  17.3 us (5%)
  other arithmetic  14.6 us (4%)
  between operations  14.1 us (4%)
    unnamed x4, waiting for transfers between devices  86.6 us
    dot_general x8, matrix products, tile_terms(): pre1 = jnp.dot(w_radial, basis, precision=lax.Precision.HIGHEST) + pair_in  47.3 us
    another operation x1, loops' own time, body(): firsts, seconds = lax.fori_loop(0, tiles.shape[0], step, start)  39.4 us
    all_gather x1, blocking collectives, body(): col_coords = lax.all_gather(coords, 'row', axis=1, tiled=True)  32.4 us
    all_gather x1, blocking collectives, body(): lax.all_gather(project(w_right, features), 'row', axis=1, tiled=True)  30.8 us
    dot_general x8, matrix products, tile_terms(): lax.dot_general(w_hidden, back2, (((0,), (0,)), ((), ())), preferred_elem...  27.5 us
    dot_general x8, matrix products, tile_terms(): lax.dot_general(w_radial, back1, (((0,), (0,)), ((), ())), precision=lax....  23.3 us
    dot_general x8, matrix products, tile_terms(): pre2 = jnp.dot(w_hidden, act1, preferred_element_type=jnp.float32)  12.6 us
  transfers between devices with their start and end apart: 2, of which 2 were waited for; matrix products, arithmetic and copies ran while one was open for 1% of the time, Pallas kernels for 0%

commit v1 on v0

v1 whole, which is shorter than its diff:
```python
import functools
import math

import jax
import jax.numpy as jnp
from jax import lax
from jax.experimental import pallas as pl
from jax.experimental.pallas import tpu as pltpu
from jax.sharding import PartitionSpec as P

CL = 128
SOFT = 0.01
RANGE = 6.0
GROUP = 8
MESH = pl.DeviceIdType.MESH
F32 = jnp.float32
BF16 = jnp.bfloat16


def peers(nrow, ncol, i, j):
    along_col = [(d, lax.rem(j + d, ncol)) for d in range(1, ncol)]
    along_row = [(d, lax.rem(i + d, nrow)) for d in range(1, nrow)]
    return along_col, along_row


def enter(i, j, along_col, along_row):
    barrier = pltpu.get_barrier_semaphore()
    for _, c in along_col:
        pl.semaphore_signal(barrier, inc=1, device_id=(i, c), device_id_type=MESH)
    for _, r in along_row:
        pl.semaphore_signal(barrier, inc=1, device_id=(r, j), device_id_type=MESH)
    return barrier, len(along_col) + len(along_row)


def gather_kernel(
    nrow, ncol, pos_ref, feat_ref, fill_ref, wl_ref, wr_ref,
    rowc_ref, rowp_ref, colc_ref, colp_ref, send_sem, recv_sem,
):
    i = lax.axis_index("row")
    j = lax.axis_index("col")
    along_col, along_row = peers(nrow, ncol, i, j)
    barrier, count = enter(i, j, along_col, along_row)
    beads = pos_ref.shape[1]
    lane = lax.broadcasted_iota(jnp.int32, (1, CL), 1)
    live = jnp.concatenate(
        [(lane < fill_ref[k]).astype(F32) for k in range(beads // CL)], 1
    )
    coords = jnp.concatenate([pos_ref[...], live, jnp.zeros((4, beads), F32)], 0)
    rowc_ref[j] = coords
    colc_ref[i] = coords
    dims = (((0,), (0,)), ((), ()))
    feats = feat_ref[...]
    rowp_ref[j] = lax.dot_general(wl_ref[...], feats, dims, preferred_element_type=F32).astype(BF16)
    colp_ref[i] = lax.dot_general(wr_ref[...], feats, dims, preferred_element_type=F32).astype(BF16)
    pl.semaphore_wait(barrier, count)
    copies = []
    for d, r in along_row:
        for ref in (colp_ref, colc_ref):
            copies.append((ref.at[i], (r, j)))
    for d, c in along_col:
        for ref in (rowp_ref, rowc_ref):
            copies.append((ref.at[j], (i, c)))
    started = []
    for k, (ref, target) in enumerate(copies):
        copy = pltpu.make_async_remote_copy(
            src_ref=ref, dst_ref=ref, send_sem=send_sem.at[k], recv_sem=recv_sem.at[k],
            device_id=target, device_id_type=MESH,
        )
        copy.start()
        started.append(copy)
    for copy in started:
        copy.wait()


def scatter_kernel(
    nrow, ncol, first_ref, second_ref, force_ref, energy_ref, row_in, col_in, send_sem, recv_sem
):
    i = lax.axis_index("row")
    j = lax.axis_index("col")
    along_col, along_row = peers(nrow, ncol, i, j)
    barrier, count = enter(i, j, along_col, along_row)
    pl.semaphore_wait(barrier, count)
    started = []
    for d, r in along_row:
        started.append((second_ref.at[r], col_in.at[d], (r, j)))
    for d, c in along_col:
        started.append((first_ref.at[c], row_in.at[d], (i, c)))
    copies = []
    for k, (src, dst, target) in enumerate(started):
        copy = pltpu.make_async_remote_copy(
            src_ref=src, dst_ref=dst, send_sem=send_sem.at[k], recv_sem=recv_sem.at[k],
            device_id=target, device_id_type=MESH,
        )
        copy.start()
        copies.append(copy)
    total = first_ref[j]
    other = second_ref[i]
    for copy in copies:
        copy.wait()
    for d in range(1, ncol):
        total = total + row_in[d]
    for d in range(1, nrow):
        other = other + col_in[d]
    force_ref[...] = total[:3] + other[:3]
    energy_ref[...] = total[3:4]


def tile_kernel(
    cpd, ncol, tiles_ref, count_ref, rowc_ref, rowp_ref, colc_ref, colp_ref,
    wrad_ref, whid_ref, wout_ref, first_ref, second_ref,
    acc_ref, left_ref, proj_ref, base_ref,
):
    row = lax.axis_index("row")
    col = lax.axis_index("col")
    hidden, nbasis = wrad_ref.shape
    clusters = acc_ref.shape[0]
    spacing = RANGE / (nbasis - 1)
    scale = math.sqrt(math.log2(math.e))
    back = -2.0 / (spacing * scale)
    live_count = count_ref[0]
    acc_ref[...] = jnp.zeros_like(acc_ref)
    second_ref[...] = jnp.zeros_like(second_ref)

    wide = jnp.concatenate(
        [0.5 * wrad_ref[...], jnp.zeros((hidden, CL - nbasis), F32)], 1
    )
    base_ref[...] = wide
    whid = whid_ref[...] * jnp.asarray(0.5, BF16)
    wout = wout_ref[...].astype(F32)
    spread = jnp.concatenate([wout] * GROUP, 1)
    spread = jnp.broadcast_to(spread, (GROUP, GROUP * hidden))
    owner = lax.broadcasted_iota(jnp.int32, (GROUP, GROUP * hidden), 1) // hidden
    which = lax.broadcasted_iota(jnp.int32, (GROUP, GROUP * hidden), 0)
    wout_wide = jnp.where(owner == which, spread, 0.0).astype(BF16)
    centers = lax.broadcasted_iota(jnp.int32, (nbasis, CL), 0).astype(F32) * scale
    lanes64 = lax.broadcasted_iota(jnp.int32, (hidden, CL), 1)
    lanes = lax.broadcasted_iota(jnp.int32, (GROUP, CL), 1)
    subl = lax.broadcasted_iota(jnp.int32, (GROUP, CL), 0)
    pick = lax.broadcasted_iota(jnp.int32, (16, 2 * CL), 0)
    side = lax.broadcasted_iota(jnp.int32, (16, 2 * CL), 1) < CL

    @pl.loop(0, live_count)
    def _(slot):
        first = tiles_ref[slot, 0]
        other = tiles_ref[slot, 1]
        col_a = first // cpd
        row_b = other // cpd
        at_a = pl.ds(pl.multiple_of(first % cpd * CL, CL), CL)
        at_b = pl.ds(pl.multiple_of(other % cpd * CL, CL), CL)
        same = jnp.logical_and(
            jnp.logical_and(col_a == col, row_b == row), first % cpd == other % cpd
        ).astype(F32)
        left = rowc_ref[col_a, :, at_a]
        left_ref[:, :8] = left.T
        proj_ref[...] = 0.5 * rowp_ref[col_a, :, at_a].astype(F32)
        right = colc_ref[row_b, :, at_b]
        pair_b = 0.5 * colp_ref[row_b, :, at_b].astype(F32)
        beads = jnp.sum(left[3:4]).astype(jnp.int32)
        chunks = (beads + GROUP - 1) // GROUP

        def chunk(c, carry):
            start = pl.multiple_of(c * GROUP, GROUP)
            mine = left_ref[pl.ds(start, GROUP), :]
            dx = mine[:, 0:1] - right[0:1]
            dy = mine[:, 1:2] - right[1:2]
            dz = mine[:, 2:3] - right[2:3]
            dist = jnp.sqrt(dx * dx + dy * dy + dz * dz + SOFT)
            mask = mine[:, 3:4] * right[3:4] * (
                1.0 - same * (subl + c * GROUP == lanes).astype(F32)
            )
            scaled = dist * (scale / spacing)
            rolled = pltpu.roll(proj_ref[...], lax.rem(nbasis - c * GROUP + CL, CL), 1)
            lhs = jnp.where(lanes64 < nbasis, base_ref[...], rolled)[:, : nbasis + 16].astype(BF16)
            lasts = []
            for a in range(GROUP):
                off = scaled[a : a + 1] - centers
                basis = jnp.exp2(-(off * off))
                lift = basis * off
                x1 = jnp.concatenate(
                    [
                        jnp.concatenate([basis, lift], 1).astype(BF16),
                        jnp.where(jnp.logical_and(pick == a, side), 1.0, 0.0).astype(BF16),
                    ],
                    0,
                )
                y1 = jnp.dot(lhs, x1, preferred_element_type=F32)
                h = y1[:, :CL] + pair_b
                t = jnp.tanh(h)
                u = 1.0 + t
                s = h * u
                d = u + s - t * s
                x2 = jnp.concatenate([s, d * y1[:, CL:]], 1).astype(BF16)
                y2 = jnp.dot(whid, x2, preferred_element_type=F32)
                h = y2[:, :CL]
                t = jnp.tanh(h)
                u = 1.0 + t
                s = h * u
                d = u + s - t * s
                lasts.append(jnp.concatenate([s, d * y2[:, CL:]], 1).astype(BF16))
            y3 = jnp.dot(wout_wide, jnp.concatenate(lasts, 0), preferred_element_type=F32)
            weight = (back * mask) * y3[:, CL:] / dist
            wx = weight * dx
            wy = weight * dy
            wz = weight * dz
            energy = jnp.sum(mask * y3[:, :CL], 1, keepdims=True)
            fx = -jnp.sum(wx, 1, keepdims=True)
            fy = -jnp.sum(wy, 1, keepdims=True)
            fz = -jnp.sum(wz, 1, keepdims=True)
            added = jnp.where(
                lanes == 0, fx, jnp.where(lanes == 1, fy, jnp.where(lanes == 2, fz, energy))
            )
            rows = pl.ds(start, GROUP)
            acc_ref[first, rows, :] = acc_ref[first, rows, :] + added
            return (carry[0] + wx, carry[1] + wy, carry[2] + wz)

        zero = jnp.zeros((GROUP, CL), F32)
        sums = lax.fori_loop(0, chunks, chunk, (zero, zero, zero))
        for k in range(3):
            total = jnp.sum(sums[k], 0, keepdims=True)
            second_ref[row_b, k : k + 1, at_b] = second_ref[row_b, k : k + 1, at_b] + total

    for k in range(clusters):
        place = (k // cpd, slice(None), slice(k % cpd * CL, k % cpd * CL + CL))
        first_ref[place] = acc_ref[k][:, :8].T


def body(nrow, ncol, positions, features, fill, tiles, tile_count, w_radial, w_left, w_right, w_hidden, w_out):
    beads = positions.shape[1]
    hidden = w_radial.shape[0]
    cpd = fill.shape[0]
    vmem = pl.BlockSpec(memory_space=pltpu.VMEM)
    smem = pl.BlockSpec(memory_space=pltpu.SMEM)
    sends = nrow + ncol - 2
    gathered = pl.pallas_call(
        functools.partial(gather_kernel, nrow, ncol),
        name="gather",
        out_shape=(
            jax.ShapeDtypeStruct((ncol, 8, beads), F32),
            jax.ShapeDtypeStruct((ncol, hidden, beads), BF16),
            jax.ShapeDtypeStruct((nrow, 8, beads), F32),
            jax.ShapeDtypeStruct((nrow, hidden, beads), BF16),
        ),
        in_specs=[vmem, vmem, smem, vmem, vmem],
        out_specs=(vmem,) * 4,
        scratch_shapes=[
            pltpu.SemaphoreType.DMA((2 * sends,)),
            pltpu.SemaphoreType.DMA((2 * sends,)),
        ],
        compiler_params=pltpu.CompilerParams(collective_id=0, has_side_effects=True),
    )(positions, features, fill, w_left, w_right)
    firsts, seconds = pl.pallas_call(
        functools.partial(tile_kernel, cpd, ncol),
        name="tiles",
        out_shape=(
            jax.ShapeDtypeStruct((ncol, 8, beads), F32),
            jax.ShapeDtypeStruct((nrow, 8, beads), F32),
        ),
        in_specs=[smem, smem] + [vmem] * 7,
        out_specs=(vmem, vmem),
        scratch_shapes=[
            pltpu.VMEM((ncol * cpd, CL, CL), F32),
            pltpu.VMEM((CL, CL), F32),
            pltpu.VMEM((hidden, CL), F32),
            pltpu.VMEM((hidden, CL), F32),
        ],
    )(tiles, tile_count, *gathered, w_radial, w_hidden, w_out[None, :])
    forces, energy = pl.pallas_call(
        functools.partial(scatter_kernel, nrow, ncol),
        name="scatter",
        out_shape=(
            jax.ShapeDtypeStruct((3, beads), F32),
            jax.ShapeDtypeStruct((1, beads), F32),
        ),
        in_specs=[vmem, vmem],
        out_specs=(vmem, vmem),
        scratch_shapes=[
            pltpu.VMEM((ncol, 8, beads), F32),
            pltpu.VMEM((nrow, 8, beads), F32),
            pltpu.SemaphoreType.DMA((sends,)),
            pltpu.SemaphoreType.DMA((sends,)),
        ],
        compiler_params=pltpu.CompilerParams(collective_id=1, has_side_effects=True),
    )(firsts, seconds)
    return forces, energy[0]


def solution(mesh):
    nrow, ncol = mesh.shape["row"], mesh.shape["col"]
    return jax.shard_map(
        functools.partial(body, nrow, ncol),
        mesh=mesh,
        in_specs=(
            P(None, ("row", "col")),
            P(None, ("row", "col")),
            P(("row", "col")),
            P(("row", "col"), None),
            P(("row", "col")),
            P(),
            P(),
            P(),
            P(),
            P(),
        ),
        out_specs=(P(None, ("row", "col")), P(("row", "col"))),
        check_vma=False,
    )
```

time: 372 us -> 112 us (0.30)
  matrix products: 125 us -> 0 us
  Pallas kernels: 0 us -> 106 us
  waiting for transfers between devices: 86.6 us -> 0 us
  blocking collectives: 73.9 us -> 0 us
  loops' own time: 39.4 us -> 0 us
  other arithmetic: 14.6 us -> 0 us
  between operations: 14.1 us -> 1.32 us
  local copies, waits for them, and re-layouts: 17.3 us -> 6.06 us
    dot_general x58 -> x0, matrix products: 125 us -> none  [the longest x8 47.3 us: tile_terms(): pre1 = jnp.dot(w_radial, basis, precision=lax.Precision.HIGHEST) + pair_in]
    pallas_call x0 -> x3, Pallas kernels: none -> 106 us  [the longest x1 46.9 us: body(): pl.pallas_call(functools.partial(scatter_kernel, nrow, ncol), name='scatt...]
    unnamed x4 -> x0, waiting for transfers between devices: 86.6 us -> none
    all_gather x4 -> x0, blocking collectives: 73.9 us -> none  [the longest x1 32.4 us: body(): col_coords = lax.all_gather(coords, 'row', axis=1, tiled=True)]
    another operation x1 -> x0, loops' own time: 39.4 us -> none  [body(): firsts, seconds = lax.fori_loop(0, tiles.shape[0], step, start)]
    dynamic_slice x16 -> x0, local copies, waits for them, and re-layouts: 11.1 us -> none  [the longest x8 11 us: step(): other = tiles[slot, 1]]
    add x9 -> x0, other arithmetic: 9.82 us -> none  [the longest x8 9.21 us: tile_terms(): proj_a.astype(jnp.float32)[:, :, None]]
  transfers between devices with their start and end apart: 2 -> 0, of which waited for: 2 -> 0; matrix products, arithmetic and copies ran while one was open for 1% -> 0% of each run, Pallas kernels for 0% -> 0%
where the time goes in v1:
time: 112 us; the launch traced here: 114 us
  Pallas kernels  106 us (95%)
  local copies, waits for them, and re-layouts  6.06 us (5%)
  between operations  1.32 us (1%)
    pallas_call x1, Pallas kernels, body(): pl.pallas_call(functools.partial(scatter_kernel, nrow, ncol), name='scatt...  46.9 us
    pallas_call x1, Pallas kernels, body(): pl.pallas_call(functools.partial(tile_kernel, cpd, ncol), name='tiles', o...  44.6 us
    pallas_call x1, Pallas kernels, body(): pl.pallas_call(functools.partial(gather_kernel, nrow, ncol), name='gather...  14.7 us
    unnamed x16, local copies, waits for them, and re-layouts  6.06 us

profile of v1, /device:TPU:0, one launch (start us, length us, event | category | flops | bytes accessed | tf_op | source)
XLA Modules:
  0.0 113.5 jit_solution(10554836321382719367)
XLA Ops:
  1.3 0.0 copy-start.3
  1.3 0.7 copy-done.3
  2.0 0.7 copy.14.tiles_ref
  2.6 0.0 copy-start
  2.6 1.4 %copy.15.wrad_ref = f32[64,32]{1,0:T(8,128)} copy(f32[64,32]{0,1:T(8,128)} %param.15) | data formatting | bytes 16384 | tf_op args[5]
  4.0 0.0 copy-done
  4.0 0.0 copy-start.1
  4.0 0.7 copy.12.wl_ref
  4.8 0.0 copy-done.1
  4.8 0.7 copy.13.wr_ref
  5.5 14.7 %gather.1 = (f32[4,8,256]{2,1,0:T(8,128)}, bf16[4,64,256]{2,1,0:T(8,128)(2,1)}, f32[8,8,256]{2,1,0:T(8,128)}, bf16[8,64,256]{2,1,0:T(8,128)(2,1)}) custom-call(f32[3,256]{1,0:T(4,128)} %pos_ref.1, bf16[128,256]{1,0:T(8,128)(2,1)} %feat_ref.1, s32[2]{0:T(128)} %fill_ref.1, bf16[128,64]{1,0:T(8,128)(2,1)} %copy.12.wl_ref, bf16[128,64]{1,0:T(8,128)(2,1)} %copy.13.wr_ref), custom_call_target="tpu_custom_call" | custom-call | tf_op jit(solution)/shard_map/gather/pallas_call | solution.py:234
  20.1 44.6 %tiles.1 = (f32[4,8,256]{2,1,0:T(8,128)}, f32[8,8,256]{2,1,0:T(8,128)}) custom-call(s32[8,2]{1,0:T(8,128)} %copy.14.tiles_ref, s32[1]{0:T(128)S(6)} %copy.18.count_ref, f32[4,8,256]{2,1,0:T(8,128)} %get-tuple-element.10.rowc_ref, bf16[4,64,256]{2,1,0:T(8,128)(2,1)} %get-tuple-element.11.rowp_ref, f32[8,8,256]{2,1,0:T(8,128)} %get-tuple-element.12.colc_ref, ...), custom_call_target="tpu_custom_call" | custom-call | tf_op jit(solution)/shard_map/tiles/pallas_call | solution.py:251
  64.7 46.9 %scatter.1 = (f32[3,256]{1,0:T(4,128)}, f32[1,256]{1,0:T(1,128)}) custom-call(f32[4,8,256]{2,1,0:T(8,128)} %get-tuple-element.14.first_ref, f32[8,8,256]{2,1,0:T(8,128)} %get-tuple-element.15.second_ref), custom_call_target="tpu_custom_call" | custom-call | tf_op jit(solution)/shard_map/scatter/pallas_call | solution.py:267
  111.6 0.0 copy-start.2
  111.7 0.7 copy-done.2
  112.3 0.0 copy-start.4
  112.3 0.6 copy.19
  112.9 0.1 copy-done.4
  113.0 0.6 copy.20
Async XLA Ops:
  1.3 0.7 copy-start.3
  2.6 1.4 %copy-start = (bf16[128,64]{0,1:T(8,128)(2,1)S(1)}, bf16[128,64]{0,1:T(8,128)(2,1)}, u32[]{:S(2)}) copy-start(bf16[128,64]{0,1:T(8,128)(2,1)} %param.16) | copy-start | bytes 49156
  4.0 0.7 copy-start.1
  111.6 0.7 copy-start.2
  112.3 0.7 copy-start.4

commit v2 on v1

--- a/solution.py
+++ b/solution.py
@@ -12,6 +12,8 @@
 SOFT = 0.01
 RANGE = 6.0
 GROUP = 8
+STEP = 16
+PICK = 16
 MESH = pl.DeviceIdType.MESH
 F32 = jnp.float32
 BF16 = jnp.bfloat16
@@ -48,7 +50,7 @@
     coords = jnp.concatenate([pos_ref[...], live, jnp.zeros((4, beads), F32)], 0)
     rowc_ref[j] = coords
     colc_ref[i] = coords
-    dims = (((0,), (0,)), ((), ()))
+    dims = (((1,), (0,)), ((), ()))
     feats = feat_ref[...]
     rowp_ref[j] = lax.dot_general(wl_ref[...], feats, dims, preferred_element_type=F32).astype(BF16)
     colp_ref[i] = lax.dot_general(wr_ref[...], feats, dims, preferred_element_type=F32).astype(BF16)
@@ -108,11 +110,11 @@
 def tile_kernel(
     cpd, ncol, tiles_ref, count_ref, rowc_ref, rowp_ref, colc_ref, colp_ref,
     wrad_ref, whid_ref, wout_ref, first_ref, second_ref,
-    acc_ref, left_ref, proj_ref, base_ref,
+    acc_ref, dist_ref, last_ref, proj_ref, pair_ref, base_ref, pick_ref,
 ):
     row = lax.axis_index("row")
     col = lax.axis_index("col")
-    hidden, nbasis = wrad_ref.shape
+    nbasis, hidden = wrad_ref.shape
     clusters = acc_ref.shape[0]
     spacing = RANGE / (nbasis - 1)
     scale = math.sqrt(math.log2(math.e))
@@ -122,7 +124,7 @@
     second_ref[...] = jnp.zeros_like(second_ref)
 
     wide = jnp.concatenate(
-        [0.5 * wrad_ref[...], jnp.zeros((hidden, CL - nbasis), F32)], 1
+        [0.5 * wrad_ref[...].T, jnp.zeros((hidden, CL - nbasis), F32)], 1
     )
     base_ref[...] = wide
     whid = whid_ref[...] * jnp.asarray(0.5, BF16)
@@ -134,15 +136,17 @@
     wout_wide = jnp.where(owner == which, spread, 0.0).astype(BF16)
     centers = lax.broadcasted_iota(jnp.int32, (nbasis, CL), 0).astype(F32) * scale
     lanes64 = lax.broadcasted_iota(jnp.int32, (hidden, CL), 1)
-    lanes = lax.broadcasted_iota(jnp.int32, (GROUP, CL), 1)
-    subl = lax.broadcasted_iota(jnp.int32, (GROUP, CL), 0)
-    pick = lax.broadcasted_iota(jnp.int32, (16, 2 * CL), 0)
-    side = lax.broadcasted_iota(jnp.int32, (16, 2 * CL), 1) < CL
+    lanes = lax.broadcasted_iota(jnp.int32, (CL, CL), 1)
+    ident = (lax.broadcasted_iota(jnp.int32, (CL, CL), 0) == lanes).astype(F32)
+    pick = lax.broadcasted_iota(jnp.int32, (PICK, 2 * CL), 0)
+    side = lax.broadcasted_iota(jnp.int32, (PICK, 2 * CL), 1) < CL
+    for a in range(STEP):
+        pick_ref[a] = jnp.where(jnp.logical_and(pick == a, side), 1.0, 0.0).astype(BF16)
 
     @pl.loop(0, live_count)
     def _(slot):
-        first = tiles_ref[slot, 0]
-        other = tiles_ref[slot, 1]
+        first = tiles_ref[0, slot]
+        other = tiles_ref[1, slot]
         col_a = first // cpd
         row_b = other // cpd
         at_a = pl.ds(pl.multiple_of(first % cpd * CL, CL), CL)
@@ -151,72 +155,68 @@
             jnp.logical_and(col_a == col, row_b == row), first % cpd == other % cpd
         ).astype(F32)
         left = rowc_ref[col_a, :, at_a]
-        left_ref[:, :8] = left.T
+        mine = left.T
         proj_ref[...] = 0.5 * rowp_ref[col_a, :, at_a].astype(F32)
         right = colc_ref[row_b, :, at_b]
-        pair_b = 0.5 * colp_ref[row_b, :, at_b].astype(F32)
+        pair_ref[...] = 0.5 * colp_ref[row_b, :, at_b].astype(F32)
         beads = jnp.sum(left[3:4]).astype(jnp.int32)
-        chunks = (beads + GROUP - 1) // GROUP
-
-        def chunk(c, carry):
-            start = pl.multiple_of(c * GROUP, GROUP)
-            mine = left_ref[pl.ds(start, GROUP), :]
-            dx = mine[:, 0:1] - right[0:1]
-            dy = mine[:, 1:2] - right[1:2]
-            dz = mine[:, 2:3] - right[2:3]
-            dist = jnp.sqrt(dx * dx + dy * dy + dz * dz + SOFT)
-            mask = mine[:, 3:4] * right[3:4] * (
-                1.0 - same * (subl + c * GROUP == lanes).astype(F32)
-            )
-            scaled = dist * (scale / spacing)
-            rolled = pltpu.roll(proj_ref[...], lax.rem(nbasis - c * GROUP + CL, CL), 1)
-            lhs = jnp.where(lanes64 < nbasis, base_ref[...], rolled)[:, : nbasis + 16].astype(BF16)
-            lasts = []
-            for a in range(GROUP):
-                off = scaled[a : a + 1] - centers
-                basis = jnp.exp2(-(off * off))
-                lift = basis * off
-                x1 = jnp.concatenate(
-                    [
-                        jnp.concatenate([basis, lift], 1).astype(BF16),
-                        jnp.where(jnp.logical_and(pick == a, side), 1.0, 0.0).astype(BF16),
-                    ],
-                    0,
+        chunks = (beads + STEP - 1) // STEP
+        dx = mine[:, 0:1] - right[0:1]
+        dy = mine[:, 1:2] - right[1:2]
+        dz = mine[:, 2:3] - right[2:3]
+        dist = jnp.sqrt(dx * dx + dy * dy + dz * dz + SOFT)
+        dist_ref[...] = dist * (scale / spacing)
+
+        @pl.loop(0, chunks)
+        def _(c):
+            start = pl.multiple_of(c * STEP, STEP)
+            rolled = pltpu.roll(proj_ref[...], lax.rem(nbasis - c * STEP + CL, CL), 1)
+            lhs = jnp.where(lanes64 < nbasis, base_ref[...], rolled)[:, : nbasis + PICK].astype(BF16)
+            for half in range(0, STEP, GROUP):
+                rows = pl.ds(pl.multiple_of(start + half, GROUP), GROUP)
+                scaled = dist_ref[rows, :]
+                lasts = []
+                for a in range(GROUP):
+                    off = scaled[a : a + 1] - centers
+                    basis = jnp.exp2(-(off * off))
+                    lift = basis * off
+                    x1 = jnp.concatenate(
+                        [jnp.concatenate([basis, lift], 1).astype(BF16), pick_ref[half + a]], 0
+                    )
+                    y1 = jnp.dot(lhs, x1, preferred_element_type=F32)
+                    h = y1[:, :CL] + pair_ref[...]
+                    t = jnp.tanh(h)
+                    u = 1.0 + t
+                    s = h * u
+                    d = u + s - t * s
+                    x2 = jnp.concatenate([s, d * y1[:, CL:]], 1).astype(BF16)
+                    y2 = jnp.dot(whid, x2, preferred_element_type=F32)
+                    h = y2[:, :CL]
+                    t = jnp.tanh(h)
+                    u = 1.0 + t
+                    s = h * u
+                    d = u + s - t * s
+                    lasts.append(jnp.concatenate([s, d * y2[:, CL:]], 1).astype(BF16))
+                last_ref[rows, :] = jnp.dot(
+                    wout_wide, jnp.concatenate(lasts, 0), preferred_element_type=F32
                 )
-                y1 = jnp.dot(lhs, x1, preferred_element_type=F32)
-                h = y1[:, :CL] + pair_b
-                t = jnp.tanh(h)
-                u = 1.0 + t
-                s = h * u
-                d = u + s - t * s
-                x2 = jnp.concatenate([s, d * y1[:, CL:]], 1).astype(BF16)
-                y2 = jnp.dot(whid, x2, preferred_element_type=F32)
-                h = y2[:, :CL]
-                t = jnp.tanh(h)
-                u = 1.0 + t
-                s = h * u
-                d = u + s - t * s
-                lasts.append(jnp.concatenate([s, d * y2[:, CL:]], 1).astype(BF16))
-            y3 = jnp.dot(wout_wide, jnp.concatenate(lasts, 0), preferred_element_type=F32)
-            weight = (back * mask) * y3[:, CL:] / dist
-            wx = weight * dx
-            wy = weight * dy
-            wz = weight * dz
-            energy = jnp.sum(mask * y3[:, :CL], 1, keepdims=True)
-            fx = -jnp.sum(wx, 1, keepdims=True)
-            fy = -jnp.sum(wy, 1, keepdims=True)
-            fz = -jnp.sum(wz, 1, keepdims=True)
-            added = jnp.where(
-                lanes == 0, fx, jnp.where(lanes == 1, fy, jnp.where(lanes == 2, fz, energy))
-            )
-            rows = pl.ds(start, GROUP)
-            acc_ref[first, rows, :] = acc_ref[first, rows, :] + added
-            return (carry[0] + wx, carry[1] + wy, carry[2] + wz)
-
-        zero = jnp.zeros((GROUP, CL), F32)
-        sums = lax.fori_loop(0, chunks, chunk, (zero, zero, zero))
-        for k in range(3):
-            total = jnp.sum(sums[k], 0, keepdims=True)
+
+        dist = dist_ref[...] * (spacing / scale)
+        both = jnp.logical_and(mine[:, 3:4] * right[3:4] > 0.5, same * ident < 0.5)
+        weight = jnp.where(both, back * last_ref[:, CL:] / dist, 0.0)
+        phi = jnp.where(both, last_ref[:, :CL], 0.0)
+        wx = weight * dx
+        wy = weight * dy
+        wz = weight * dz
+        energy = jnp.sum(phi, 1, keepdims=True)
+        fx = -jnp.sum(wx, 1, keepdims=True)
+        fy = -jnp.sum(wy, 1, keepdims=True)
+        fz = -jnp.sum(wz, 1, keepdims=True)
+        acc_ref[first] = acc_ref[first] + jnp.where(
+            lanes == 0, fx, jnp.where(lanes == 1, fy, jnp.where(lanes == 2, fz, energy))
+        )
+        for k, part in enumerate((wx, wy, wz)):
+            total = jnp.sum(part, 0, keepdims=True)
             second_ref[row_b, k : k + 1, at_b] = second_ref[row_b, k : k + 1, at_b] + total
 
     for k in range(clusters):
@@ -247,7 +247,7 @@
             pltpu.SemaphoreType.DMA((2 * sends,)),
         ],
         compiler_params=pltpu.CompilerParams(collective_id=0, has_side_effects=True),
-    )(positions, features, fill, w_left, w_right)
+    )(positions, features, fill, w_left.T, w_right.T)
     firsts, seconds = pl.pallas_call(
         functools.partial(tile_kernel, cpd, ncol),
         name="tiles",
@@ -260,10 +260,13 @@
         scratch_shapes=[
             pltpu.VMEM((ncol * cpd, CL, CL), F32),
             pltpu.VMEM((CL, CL), F32),
+            pltpu.VMEM((CL, 2 * CL), F32),
             pltpu.VMEM((hidden, CL), F32),
             pltpu.VMEM((hidden, CL), F32),
+            pltpu.VMEM((hidden, CL), F32),
+            pltpu.VMEM((STEP, PICK, 2 * CL), BF16),
         ],
-    )(tiles, tile_count, *gathered, w_radial, w_hidden, w_out[None, :])
+    )(tiles.T, tile_count, *gathered, w_radial.T, w_hidden, w_out[None, :])
     forces, energy = pl.pallas_call(
         functools.partial(scatter_kernel, nrow, ncol),
         name="scatter",

time: 112 us -> 97.7 us (0.87)
  Pallas kernels: 106 us -> 95.5 us
  local copies, waits for them, and re-layouts: 6.06 us -> 1.9 us
    pallas_call x1, Pallas kernels: 44.6 us -> 20.5 us  [body(): pl.pallas_call(functools.partial(tile_kernel, cpd, ncol), name='tiles', o...]
    pallas_call x1, Pallas kernels: 46.9 us -> 60.3 us  [body(): pl.pallas_call(functools.partial(scatter_kernel, nrow, ncol), name='scatt...]
    unnamed x16 -> x6, local copies, waits for them, and re-layouts: 6.06 us -> 1.9 us
where the time goes in v2:
time: 97.7 us; the launch traced here: 98.7 us
  Pallas kernels  95.5 us (98%)
  local copies, waits for them, and re-layouts  1.9 us (2%)
  between operations  1.3 us (1%)
    pallas_call x1, Pallas kernels, body(): pl.pallas_call(functools.partial(scatter_kernel, nrow, ncol), name='scatt...  60.3 us
    pallas_call x1, Pallas kernels, body(): pl.pallas_call(functools.partial(tile_kernel, cpd, ncol), name='tiles', o...  20.5 us
    pallas_call x1, Pallas kernels, body(): pl.pallas_call(functools.partial(gather_kernel, nrow, ncol), name='gather...  14.7 us

profile of v2, /device:TPU:0, one launch (start us, length us, event | category | flops | bytes accessed | tf_op | source)
XLA Modules:
  0.0 98.7 jit_solution(1160826861813820214)
XLA Ops:
  1.3 14.7 %gather.1 = (f32[4,8,256]{2,1,0:T(8,128)}, bf16[4,64,256]{2,1,0:T(8,128)(2,1)}, f32[8,8,256]{2,1,0:T(8,128)}, bf16[8,64,256]{2,1,0:T(8,128)(2,1)}) custom-call(f32[3,256]{1,0:T(4,128)} %pos_ref.1, bf16[128,256]{1,0:T(8,128)(2,1)} %feat_ref.1, s32[2]{0:T(128)} %fill_ref.1, bf16[64,128]{1,0:T(8,128)(2,1)} %bitcast.6, bf16[64,128]{1,0:T(8,128)(2,1)} %bitcast.7), custom_call_target="tpu_custom_call" | custom-call | tf_op jit(solution)/shard_map/gather/pallas_call | solution.py:234
  16.0 20.5 %tiles.1 = (f32[4,8,256]{2,1,0:T(8,128)}, f32[8,8,256]{2,1,0:T(8,128)}) custom-call(s32[2,8]{1,0:T(2,128)} %bitcast.9, s32[1]{0:T(128)S(6)} %copy.14.count_ref, f32[4,8,256]{2,1,0:T(8,128)} %get-tuple-element.10.rowc_ref, bf16[4,64,256]{2,1,0:T(8,128)(2,1)} %get-tuple-element.11.rowp_ref, f32[8,8,256]{2,1,0:T(8,128)} %get-tuple-element.12.colc_ref, ...), custom_call_target="tpu_custom_call" | custom-call | tf_op jit(solution)/shard_map/tiles/pallas_call | solution.py:251
  36.5 60.3 %scatter.1 = (f32[3,256]{1,0:T(4,128)}, f32[1,256]{1,0:T(1,128)}) custom-call(f32[4,8,256]{2,1,0:T(8,128)} %get-tuple-element.14.first_ref, f32[8,8,256]{2,1,0:T(8,128)} %get-tuple-element.15.second_ref), custom_call_target="tpu_custom_call" | custom-call | tf_op jit(solution)/shard_map/scatter/pallas_call | solution.py:270
  96.8 0.0 copy-start
  96.8 0.7 copy-done
  97.5 0.0 copy-start.1
  97.5 0.6 copy.15
  98.1 0.1 copy-done.1
  98.2 0.6 copy.16
Async XLA Ops:
  96.8 0.7 copy-start
  97.5 0.7 copy-start.1
